TPU v7x, 128 devices: a whole 4x4x4 slice. The times are simulated.
128 devices in a mesh: section: 2 (over z_lo), patch: 4 (over y), shard: 16 (over z_hi, x, core).
Axes of the slice: x: 4, y: 4, z: 4 (z_hi: 2, z_lo: 2; z = z_hi * 2 + z_lo), core: 2. Of those that a mesh axis runs over, the one named last changes fastest.
Arguments:
- hidden: bfloat16 [32, 1024, 2432], P('shard', 'patch'), may hold values from -6 to 6
- text_kv: bfloat16 [2, 32, 154, 2432], P('section', 'shard'), may hold values from -6 to 6, as said below
- stale_kv: bfloat16 [2, 32, 1024, 2432], P('section', 'shard', 'patch'), may hold values from -6 to 6, as said below
- modulation: float32 [2, 32, 3, 2432], P('section', 'shard'), may hold values from -3 to 3
- score_gain: float32 [2, 64], P('section'), may hold values from 1.5 to 4
- qkv_weight: bfloat16 [2, 2432, 3648], P('section', 'shard'), may hold values from -0.125 to 0.125
- out_weight: bfloat16 [2, 1216, 2432], P('section', None, 'shard'), may hold values from -0.15625 to 0.15625
- final_mod: float32 [32, 2, 2432], P('shard'), may hold values from -3 to 3
- final_weight: bfloat16 [2432, 64], replicated, may hold values from -0.125 to 0.125
- latent: float32 [32, 1024, 64], P('shard', ('patch', 'section')), may hold values from -6 to 6
- step_index: int32 [32], P('shard'), may hold values from 0 to 27
Outputs:
- new_kv: bfloat16 [2, 32, 1024, 2432], P('section', 'shard', 'patch')
- latent_next: float32 [32, 1024, 64], P('shard', ('patch', 'section'))
- denoised: float32 [32, 1024, 64], P('shard', ('patch', 'section'))
Inputs may be any that keep to these rules, and one draw needn't show every extreme that they name: `text_kv`: in every row the first 1216 columns are 19 heads of 64 key features, each head with mean square one up to bfloat16 rounding. `stale_kv`: in every row the first 1216 columns are 19 heads of 64 key features, each head with mean square one up to bfloat16 rounding.
All inputs are finite; a program needn't handle non-finite values.
Results may differ from a plain program's by a relative error of at most 0.008.
Values may be sent and summed in bfloat16 or wider, within the bound.
No kernel may reach another device: no remote copies, remote signals or barrier semaphores. Data moves between devices by JAX's collectives and lax.ppermute only.
A program may use at most 192 MiB of HBM per device.

v0:
```python
import math
import jax
import jax.numpy as jnp
from jax import lax
from jax.sharding import PartitionSpec as P

HEAD = 64
NSTEPS = 28
eps_norm = 1e-06
flow_shift = 3.0


def passed_along(value, axis, steps):
    count = lax.axis_size(axis)
    first, last = (max(0, -steps), min(count, count - steps))
    return lax.ppermute(value, axis, [(source, source + steps) for source in range(first, last)])


def spread(array, axis, root):
    mine = lax.axis_index(axis) == root
    return lax.psum(jnp.where(mine, array, jnp.zeros_like(array)), axis)


def sigma_of(step):
    s = 1.0 - step.astype(jnp.float32) / NSTEPS
    return flow_shift * s / (1.0 + (flow_shift - 1.0) * s)


def modulated(xf, shift, scale):
    mean = jnp.mean(xf, -1, keepdims=True)
    cent = xf - mean
    var = jnp.mean(cent * cent, -1, keepdims=True)
    return cent * lax.rsqrt(var + eps_norm) * (1.0 + scale) + shift


def attend_one(query, keys_all, width, heads):
    count = keys_all.shape[0]
    keys = keys_all[:, :width].reshape(count, heads, HEAD)
    values = keys_all[:, width:].reshape(count, heads, HEAD)
    scores = jnp.einsum("qhe,khe->hqk", query, keys, preferred_element_type=jnp.float32)
    expo = jnp.exp(scores)
    total = jnp.sum(expo, -1)
    weights = expo.astype(jnp.bfloat16)
    mixed = jnp.einsum("hqk,khe->qhe", weights, values, preferred_element_type=jnp.float32)
    mixed = mixed / jnp.transpose(total)[:, :, None]
    return mixed.reshape(query.shape[0], width).astype(jnp.bfloat16)


def run_layer(x, stale_all, text_one, mod_one, gain, w_qkv, w_out, patch_index):
    requests, rows = (x.shape[0], x.shape[1])
    width = w_out.shape[0]
    heads = width // HEAD
    xf = x.astype(jnp.float32)
    normed = modulated(xf, mod_one[:, 0:1, :], mod_one[:, 1:2, :]).astype(jnp.bfloat16)
    proj_in = jnp.einsum("rid,dc->ric", normed, w_qkv, preferred_element_type=jnp.float32)
    q = proj_in[..., :width].reshape(requests, rows, heads, HEAD)
    k = proj_in[..., width : 2 * width].reshape(requests, rows, heads, HEAD)
    v = proj_in[..., 2 * width :]
    q_hat = q * lax.rsqrt(jnp.mean(q * q, -1, keepdims=True) + eps_norm)
    k_hat = k * lax.rsqrt(jnp.mean(k * k, -1, keepdims=True) + eps_norm)
    fresh = jnp.concatenate(
        [k_hat.reshape(requests, rows, width).astype(jnp.bfloat16), v.astype(jnp.bfloat16)], -1
    )
    query = (q_hat * gain / math.sqrt(HEAD)).astype(jnp.bfloat16)
    mixed = lax.dynamic_update_slice_in_dim(stale_all, fresh, patch_index * rows, 1)
    keys_all = jnp.concatenate([text_one, mixed], 1)

    def per_request(pair):
        return attend_one(pair[0], pair[1], width, heads)

    attn = lax.map(per_request, (query, keys_all))
    proj = jnp.einsum("riw,wd->rid", attn, w_out, preferred_element_type=jnp.float32)
    x_next = (xf + mod_one[:, 2:3, :] * proj).astype(jnp.bfloat16)
    return (x_next, fresh)


def on_device(
    hidden,
    text_kv,
    stale_kv,
    modulation,
    score_gain,
    qkv_weight,
    out_weight,
    final_mod,
    final_weight,
    latent,
    step_index,
):
    w_qkv, w_out = (
        lax.all_gather(qkv_weight[0], "shard", axis=0, tiled=True),
        lax.all_gather(out_weight[0], "shard", axis=1, tiled=True),
    )
    stale_all = lax.all_gather(stale_kv[0], "patch", axis=1, tiled=True)
    section = lax.axis_index("section")
    patch_index = lax.axis_index("patch")

    def compute(x):
        return run_layer(
            x, stale_all, text_kv[0], modulation[0], score_gain[0], w_qkv, w_out, patch_index
        )

    def passing(x):
        return (x, jnp.zeros(stale_kv.shape[1:], jnp.bfloat16))

    first, fresh_first = lax.cond(section == 0, compute, passing, hidden)
    arrived = passed_along(first, "section", 1)
    last, fresh_last = lax.cond(section == 1, compute, passing, arrived)
    fresh = jnp.where(section == 0, fresh_first, fresh_last)
    final = modulated(last.astype(jnp.float32), final_mod[:, 0:1, :], final_mod[:, 1:2, :]).astype(
        jnp.bfloat16
    )
    velocity = jnp.einsum("rid,dc->ric", final, final_weight, preferred_element_type=jnp.float32)
    half = latent.shape[1]
    shared = spread(velocity.astype(jnp.bfloat16), "section", 1).astype(velocity.dtype)
    velocity_mine = lax.dynamic_slice_in_dim(shared, section * half, half, 1)
    sig = sigma_of(step_index)[:, None, None]
    sig_next = sigma_of(step_index + 1)[:, None, None]
    latent_next = latent + (sig_next - sig) * velocity_mine
    denoised = latent - sig * velocity_mine
    return (fresh[None], latent_next, denoised)


def solution(mesh):
    in_specs = (
        P("shard", "patch", None),
        P("section", "shard", None, None),
        P("section", "shard", "patch", None),
        P("section", "shard", None, None),
        P("section", None),
        P("section", "shard", None),
        P("section", None, "shard"),
        P("shard", None, None),
        P(),
        P("shard", ("patch", "section"), None),
        P("shard"),
    )
    out_specs = (
        P("section", "shard", "patch", None),
        P("shard", ("patch", "section"), None),
        P("shard", ("patch", "section"), None),
    )
    return jax.shard_map(
        on_device, mesh=mesh, in_specs=in_specs, out_specs=out_specs, check_vma=False
    )
```

profile of v0, /device:TPU:1, one launch (start us, length us, event | category | flops | bytes accessed | tf_op | source)
XLA Modules:
  0.0 642.9 jit_solution(3232019068005679391)
XLA Ops:
  7.2 0.0 copy-start
  7.2 0.0 all-gather.11.cloned.1.call-start
  7.2 0.7 all-gather.11.cloned.1.call-update
  7.9 0.0 copy-start.2
  7.9 0.0 copy-start.7
  7.9 0.0 all-gather.9.cloned.1.call-start
  8.0 4.5 copy.28
  12.5 0.0 all-gather.9.cloned.1.call-update
  12.5 0.0 all-gather.7.cloned.1.call-start
  12.5 0.7 all-gather.7.cloned.1.call-update
  13.2 0.0 all-reduce.2.cloned.1.call-start
  13.3 64.7 %all-gather.11.cloned.1.call-done = bf16[1,1216,2432]{1,2,0:T(8,128)(2,1)} async-done(((bf16[1,1216,152]{1,2,0:T(8,128)(2,1)}), bf16[1,1216,2432]{1,2,0:T(8,128)(2,1)}) %all-gather.11.cloned.1.call-update) | async-done | bytes 5914640 | tf_op jit(solution)/shard_map/all_gather | solution.py:92
  78.0 100.0 %all-gather.9.cloned.1.call-done = bf16[1,2,1024,2432]{2,3,1,0:T(8,128)(2,1)} async-done(((bf16[1,2,256,2432]{2,3,1,0:T(8,128)(2,1)}), bf16[1,2,1024,2432]{2,3,1,0:T(8,128)(2,1)}) %all-gather.9.cloned.1.call-update) | async-done | bytes 9961488 | tf_op jit(solution)/shard_map/all_gather | solution.py:94
  177.9 120.4 %all-gather.7.cloned.1.call-done = bf16[1,2432,3648]{2,1,0:T(8,128)(2,1)} async-done(((bf16[1,152,3648]{2,1,0:T(8,128)(2,1)}), bf16[1,2432,3648]{2,1,0:T(8,128)(2,1)}) %all-gather.7.cloned.1.call-update) | async-done | bytes 17743888 | tf_op jit(solution)/shard_map/all_gather | solution.py:91
  298.4 0.0 copy-start.9
  298.4 129.6 %conditional.2 = (bf16[2,256,2432]{2,1,0:T(8,128)(2,1)S(1)}, bf16[2,256,2432]{2,1,0:T(8,128)(2,1)}) conditional(s32[]{:T(128)} %convert_element_type.88, bf16[2,256,2432]{2,1,0:T(8,128)(2,1)S(1)} %copy-done.2, (bf16[2,256,2432]{2,1,0:T(8,128)(2,1)S(1)}, f32[1,2,3,2432]{3,1,2,0:T(2,128)S(1)}, bf16[2432,3648]{1,0:T(8,128)(2,1)}, f32[1,64]{1,0:T(1,128)S(1)}, ...), branch_computations={%region_0.0_spmd, %region_1.9_spmd} | conditional | flops 13646128128 | bytes 220811024 | solution.py:106
  298.4 0.4 convert_reduce_fusion
  298.8 0.8 fusion.15
  299.6 0.6 slice_bitcast_fusion.1
  300.2 16.5 %fusion.6 = f32[2,256,3648]{1,2,0:T(8,128)} fusion(bf16[2432,3648]{1,0:T(8,128)(2,1)} %get-tuple-element.139, bf16[2,256,2432]{2,1,0:T(8,128)(2,1)S(1)} %get-tuple-element.71, f32[2,2432]{1,0:T(2,128)S(1)} %get-tuple-element.182, f32[2,2432]{1,0:T(2,128)S(1)} %get-tuple-element.183, f32[2,256]{1,0:T(2,128)S(1)} %add_rsqrt_fusion.2, ...), kind=kOutput, calls=%fused_computation.11 | convolution fusion | flops 9092333568 | bytes 27748352 | tf_op jit(solution)/shard_map/cond/branch_1_fun/rid,dc->ric/dot_general | solution.py:55
  316.7 3.3 slice_multiply_fusion
  320.1 2.0 reduce_sum.99
  322.1 4.7 fusion.76
  326.7 2.9 slice.91
  329.6 8.8 %copy.62 = bf16[2,1024,2432]{1,2,0:T(8,128)(2,1)} copy(bf16[2,1024,2432]{1,2,0:T(8,128)(2,1)} %get-tuple-element.74) | data formatting | bytes 19922944 | tf_op jit(solution)/shard_map/cond
  338.4 4.3 pad_maximum_fusion.1
  342.7 5.8 copy.30
  348.5 13.1 %pad_maximum_fusion = bf16[2,1178,2432]{1,2,0:T(8,128)(2,1)} fusion(bf16[2,1024,2432]{1,2,0:T(8,128)(2,1)} %get-tuple-element.180, bf16[2,154,2432]{1,2,0:T(8,128)(2,1)} %bitcast.147), kind=kLoop, calls=%fused_computation.13 | loop fusion | flops 22919168 | bytes 22919168 | tf_op jit(solution)/shard_map/cond/branch_1_fun/concatenate | solution.py:66
  361.6 0.3 multiply_reduce_fusion
  361.9 1.5 multiply_convert_fusion
  363.5 52.4 %while.18 = (s32[]{:T(128)}, bf16[2,256,1216]{1,2,0:T(8,128)(2,1)}, bf16[2,1178,2432]{1,2,0:T(8,128)(2,1)}, bf16[2,256,19,64]{1,3,2,0:T(8,128)(2,1)}, s32[]{:T(128)}) while((s32[]{:T(128)}, bf16[2,256,1216]{1,2,0:T(8,128)(2,1)}, bf16[2,1178,2432]{1,2,0:T(8,128)(2,1)}, bf16[2,256,19,64]{1,3,2,0:T(8,128)(2,1)}, s32[]{:T(128)}) %tuple.88), condition=%wide.region_8.8_spmd, body=%wide.region_6.7_spmd.sunk | while | flops 1478904064 | bytes 82245984 | solution.py:71
  364.0 3.2 dynamic-slice_bitcast_fusion.5
  367.1 0.0 copy-start.5
  367.2 0.4 fusion.96
  367.6 0.9 copy-done.5
  368.4 9.7 %exponential_reduce_fusion.5 = (f32[19,256]{1,0:T(8,128)S(1)}, f32[19,256,1178]{1,2,0:T(8,128)}) fusion(bf16[1178,19,64]{0,2,1:T(8,128)(2,1)S(1)} %bitcast.134, bf16[2,256,19,64]{1,3,2,0:T(8,128)(2,1)S(1)} %copy-done.5, s32[]{:T(128)} %get-tuple-element.287), kind=kOutput, calls=%fused_computation.clone.1 | convolution fusion | flops 739138304 | bytes 26674180 | tf_op jit(solution)/shard_map/cond/branch_1_fun/while/body/eval_jaxpr/qhe,khe->hqk/dot_general | solution.py:40
  378.1 10.9 %divide_convert_fusion.5 = bf16[256,19,64]{0,2,1:T(8,128)(2,1)S(1)} fusion(bf16[1178,19,64]{0,2,1:T(8,128)(2,1)S(1)} %bitcast.136, f32[19,256,1178]{1,2,0:T(8,128)} %get-tuple-element.265, f32[256,19]{0,1:T(8,128)S(1)} %bitcast.150), kind=kOutput, calls=%fused_computation.5.clone.1 | convolution fusion | flops 739765760 | bytes 26426112 | tf_op jit(solution)/shard_map/cond/branch_1_fun/while/body/eval_jaxpr/hqk,khe->qhe/dot_general | solution.py:44
  389.0 0.9 constant_dynamic-update-slice_fusion.7
  389.9 3.2 dynamic-slice_bitcast_fusion.5
  393.1 0.4 fusion.96
  393.5 0.9 copy-done.5
  394.4 9.7 %exponential_reduce_fusion.5 = (f32[19,256]{1,0:T(8,128)S(1)}, f32[19,256,1178]{1,2,0:T(8,128)}) fusion(bf16[1178,19,64]{0,2,1:T(8,128)(2,1)S(1)} %bitcast.134, bf16[2,256,19,64]{1,3,2,0:T(8,128)(2,1)S(1)} %copy-done.5, s32[]{:T(128)} %get-tuple-element.287), kind=kOutput, calls=%fused_computation.clone.1 | convolution fusion | flops 739138304 | bytes 26674180 | tf_op jit(solution)/shard_map/cond/branch_1_fun/while/body/eval_jaxpr/qhe,khe->hqk/dot_general | solution.py:40
  404.1 10.9 %divide_convert_fusion.5 = bf16[256,19,64]{0,2,1:T(8,128)(2,1)S(1)} fusion(bf16[1178,19,64]{0,2,1:T(8,128)(2,1)S(1)} %bitcast.136, f32[19,256,1178]{1,2,0:T(8,128)} %get-tuple-element.265, f32[256,19]{0,1:T(8,128)S(1)} %bitcast.150), kind=kOutput, calls=%fused_computation.5.clone.1 | convolution fusion | flops 739765760 | bytes 26426112 | tf_op jit(solution)/shard_map/cond/branch_1_fun/while/body/eval_jaxpr/hqk,khe->qhe/dot_general | solution.py:44
  415.0 0.9 constant_dynamic-update-slice_fusion.7
  415.9 7.6 %fusion.19 = bf16[2,256,2432]{2,1,0:T(8,128)(2,1)S(1)} fusion(bf16[2,256,2432]{2,1,0:T(8,128)(2,1)S(1)} %get-tuple-element.71, bf16[2,256,1216]{1,2,0:T(8,128)(2,1)} %get-tuple-element.78, bf16[1216,2432]{0,1:T(8,128)(2,1)} %get-tuple-element.144, f32[2,2432]{1,0:T(2,128)S(1)} %copy-done.10), kind=kOutput, calls=%fused_computation.26 | convolution fusion | flops 3033268224 | bytes 12160000 | tf_op jit(solution)/shard_map/cond/branch_1_fun/riw,wd->rid/dot_general | solution.py:72
  423.5 4.3 copy.46
  428.0 1.5 copy-done.1
  429.4 1.4 collective-permute-start
  430.9 0.6 divide_subtract_fusion
  431.5 0.6 copy_bitcast_fusion
  432.2 52.4 %collective-permute-done = bf16[2,256,2432]{2,1,0:T(8,128)(2,1)S(1)} collective-permute-done((bf16[2,256,2432]{2,1,0:T(8,128)(2,1)}, bf16[2,256,2432]{2,1,0:T(8,128)(2,1)S(1)}, u32[]{:S(2)}, u32[]{:S(2)}) %collective-permute-start) | collective-permute-done | bytes 2490400 | tf_op jit(solution)/shard_map/ppermute | solution.py:16
  484.6 4.3 conditional.3
  484.6 1.6 broadcast.161.clone
  488.9 0.0 copy-start.12
  488.9 0.0 copy-start.13
  488.9 0.4 convert_reduce_fusion.2
  489.3 0.8 fusion.60
  490.2 1.8 fusion.69
  492.0 0.0 all-reduce.2.cloned.1.call-update
  492.0 0.0 copy-start.8
  492.0 3.4 select_bitcast_fusion
  495.5 138.9 %all-reduce.2.cloned.1.call-done = bf16[2,256,64]{1,2,0:T(8,128)(2,1)} async-done(((bf16[2,256,64]{1,2,0:T(8,128)(2,1)}), bf16[2,256,64]{1,2,0:T(8,128)(2,1)}) %all-reduce.2.cloned.1.call-update) | async-done | bytes 65552 | tf_op jit(solution)/shard_map/psum | solution.py:21
  634.4 0.0 copy-done.15
  634.4 1.5 fusion.73
  (28 shorter events, 0.1 us)
Async XLA Ops:
  7.2 483.0 %copy-start = (bf16[2432,64]{0,1:T(8,128)(2,1)S(1)}, bf16[2432,64]{0,1:T(8,128)(2,1)}, u32[]{:S(2)}) copy-start(bf16[2432,64]{0,1:T(8,128)(2,1)} %param.27) | copy-start | bytes 933892
  7.2 70.8 %all-gather.11.cloned.1.call-start = ((), (), s32[]{:S(2)}) async-start(), calls=%async_computation.3 | async-start | bytes 6615040 | tf_op jit(solution)/shard_map/all_gather | solution.py:92
  7.9 290.4 %copy-start.2 = (bf16[2,256,2432]{2,1,0:T(8,128)(2,1)S(1)}, bf16[2,256,2432]{2,1,0:T(8,128)(2,1)}, u32[]{:S(2)}) copy-start(bf16[2,256,2432]{2,1,0:T(8,128)(2,1)} %param.19) | copy-start | bytes 7471108
  7.9 290.4 %copy-start.7 = (f32[1,2,3,2432]{3,1,2,0:T(2,128)S(1)}, f32[1,2,3,2432]{3,1,2,0:T(2,128)}, u32[]{:S(2)}) copy-start(f32[1,2,3,2432]{3,1,2,0:T(2,128)} %param.22) | copy-start | bytes 175108
  7.9 290.4 %copy-start.14 = (f32[1,64]{1,0:T(1,128)S(1)}, f32[1,64]{1,0:T(1,128)}, u32[]{:S(2)}) copy-start(f32[1,64]{1,0:T(1,128)} %param.23) | copy-start | bytes 772
  7.9 170.0 %all-gather.9.cloned.1.call-start = ((), (), s32[]{:S(2)}) async-start(), calls=%async_computation.2 | async-start | bytes 12451840 | tf_op jit(solution)/shard_map/all_gather | solution.py:94
  12.5 285.9 %all-gather.7.cloned.1.call-start = ((), (), s32[]{:S(2)}) async-start(), calls=%async_computation.1 | async-start | bytes 19183616 | tf_op jit(solution)/shard_map/all_gather | solution.py:91
  13.2 621.2 %all-reduce.2.cloned.1.call-start = ((), (), s32[]{:S(2)}) async-start(), calls=%async_computation | async-start | bytes 131072 | tf_op jit(solution)/shard_map/psum | solution.py:21
  298.4 132.5 %copy-start.17 = (s32[2]{0:T(128)S(1)}, s32[2]{0:T(128)}, u32[]{:S(2)}) copy-start(s32[2]{0:T(128)} %param.29) | copy-start | bytes 28
  298.4 133.1 %copy-start.9 = (f32[2,2,2432]{2,1,0:T(2,128)S(1)}, f32[2,2,2432]{2,1,0:T(2,128)}, u32[]{:S(2)}) copy-start(f32[2,2,2432]{2,1,0:T(2,128)} %param.26) | copy-start | bytes 116740
  348.5 13.1 %copy-start.3 = (f32[2,256,1216]{1,2,0:T(8,128)S(1)}, f32[2,256,1216]{1,2,0:T(8,128)}, u32[]{:S(2)}) copy-start(f32[2,256,1216]{1,2,0:T(8,128)} %get-tuple-element.177) | copy-start | bytes 7471108 | tf_op jit(solution)/shard_map/cond
  363.5 52.4 %copy-start.10 = (f32[2,2432]{1,0:T(2,128)S(1)}, f32[2,2432]{1,0:T(2,128)}, u32[]{:S(2)}) copy-start(f32[2,2432]{1,0:T(2,128)} %get-tuple-element.181) | copy-start | bytes 58372 | tf_op jit(solution)/shard_map/cond
  367.1 1.3 copy-start.5
  393.1 1.3 copy-start.5
  428.0 1.5 copy-start.1
  429.4 55.1 %collective-permute-start = (bf16[2,256,2432]{2,1,0:T(8,128)(2,1)}, bf16[2,256,2432]{2,1,0:T(8,128)(2,1)S(1)}, u32[]{:S(2)}, u32[]{:S(2)}) collective-permute-start(bf16[2,256,2432]{2,1,0:T(8,128)(2,1)} %copy-done.1), channel_id=1, source_target_pairs={{0,64},{1,65},{2,66},{3,67},{4,68},{5,69},{6,70},{7,71},{8,72},{9,... | collective-permute-start | bytes 7471112 | tf_op jit(solution)/shard_map/ppermute | solution.py:16
  488.9 1.2 copy-start.12
  488.9 1.2 copy-start.13
  492.0 142.4 %copy-start.8 = (f32[2,128,64]{1,2,0:T(8,128)S(1)}, f32[2,128,64]{1,2,0:T(8,128)}, u32[]{:S(2)}) copy-start(f32[2,128,64]{1,2,0:T(8,128)} %param.28) | copy-start | bytes 196612
  492.0 142.4 %copy-start.15 = (f32[2]{0:T(128)S(1)}, f32[2]{0:T(128)}, u32[]{:S(2)}) copy-start(f32[2]{0:T(128)} %get-tuple-element.171) | copy-start | bytes 28
  492.0 142.4 %copy-start.16 = (f32[2]{0:T(128)S(1)}, f32[2]{0:T(128)}, u32[]{:S(2)}) copy-start(f32[2]{0:T(128)} %get-tuple-element.172) | copy-start | bytes 28
Sparse Core Ops, SparseCore 0:
  10.4 67.5 all-gather.10
  80.2 97.6 all-gather.8
  180.5 117.8 all-gather.6
  492.1 142.2 all-reduce.1
where the time goes:
time: 652 us; the launch traced here: 643 us
  waiting for transfers between devices  478 us (73%)
  matrix products  67.2 us (10%)
  local copies, waits for them, and re-layouts  40.7 us (6%)
  other arithmetic  37.8 us (6%)
  between operations  14.4 us (2%)
    psum x1, waiting for transfers between devices, spread(): return lax.psum(jnp.where(mine, array, jnp.zeros_like(array)), axis)  139 us
    all_gather x1, waiting for transfers between devices, on_device(): lax.all_gather(qkv_weight[0], 'shard', axis=0, tiled=True)  120 us
    all_gather x1, waiting for transfers between devices, on_device(): stale_all = lax.all_gather(stale_kv[0], 'patch', axis=1, tiled=True)  100 us
    all_gather x1, waiting for transfers between devices, on_device(): lax.all_gather(out_weight[0], 'shard', axis=1, tiled=True)  64.7 us
    ppermute x1, waiting for transfers between devices, passed_along(): lax.ppermute(value, axis, [(source, source + steps) for source in range(f...  52.4 us
    dot_general x2, matrix products, attend_one(): jnp.einsum('hqk,khe->qhe', weights, values, preferred_element_type=jnp.fl...  21.8 us
    dot_general x2, matrix products, attend_one(): jnp.einsum('qhe,khe->hqk', query, keys, preferred_element_type=jnp.float32)  19.4 us
    dot_general x1, matrix products, run_layer(): jnp.einsum('rid,dc->ric', normed, w_qkv, preferred_element_type=jnp.float32)  16.5 us
  transfers between devices with their start and end apart: 5, of which 5 were waited for; matrix products, arithmetic and copies ran while one was open for 1% of the time, Pallas kernels for 0%

commit v1 on v0

--- a/solution.py
+++ b/solution.py
@@ -91,7 +91,14 @@
         lax.all_gather(qkv_weight[0], "shard", axis=0, tiled=True),
         lax.all_gather(out_weight[0], "shard", axis=1, tiled=True),
     )
-    stale_all = lax.all_gather(stale_kv[0], "patch", axis=1, tiled=True)
+    own = stale_kv[0]
+    count_2 = lax.axis_size("patch")
+    held, parts = (own, [own])
+    for _ in range(count_2 - 1):
+        held = lax.ppermute(held, "patch", [(i, (i + 1) % count_2) for i in range(count_2)])
+        parts.insert(0, held)
+    line = jnp.concatenate(parts, axis=1)
+    stale_all = jnp.roll(line, (lax.axis_index("patch") + 1) * own.shape[1], axis=1)
     section = lax.axis_index("section")
     patch_index = lax.axis_index("patch")
 

time: 652 us -> 561 us (0.86)
  waiting for transfers between devices: 478 us -> 359 us
  local copies, waits for them, and re-layouts: 40.7 us -> 70.4 us
    ppermute x0 -> x3, waiting for transfers between devices: none -> 165 us  [on_device(): lax.ppermute(held, 'patch', [(i, (i + 1) % count_2) for i in range(count_...]
    all_gather x1, waiting for transfers between devices: 120 us -> 0.01 us  [on_device(): lax.all_gather(qkv_weight[0], 'shard', axis=0, tiled=True)]
    all_gather x1 -> x0, waiting for transfers between devices: 100 us -> none  [on_device(): stale_all = lax.all_gather(stale_kv[0], 'patch', axis=1, tiled=True)]
    all_gather x1, waiting for transfers between devices: 64.7 us -> 0.01 us  [on_device(): lax.all_gather(out_weight[0], 'shard', axis=1, tiled=True)]
    unnamed x26 -> x37, local copies, waits for them, and re-layouts: 6.62 us -> 25.6 us
    dynamic_slice x0 -> x1, local copies, waits for them, and re-layouts: none -> 8.88 us  [on_device(): jnp.roll(line, (lax.axis_index('patch') + 1) * own.shape[1], axis=1)]
  transfers between devices with their start and end apart: 5 -> 7, of which waited for: 5 -> 5; matrix products, arithmetic and copies ran while one was open for 1% -> 7% of each run, Pallas kernels for 0% -> 0%
where the time goes in v1:
time: 561 us; the launch traced here: 556 us
  waiting for transfers between devices  359 us (64%)
  local copies, waits for them, and re-layouts  70.4 us (13%)
  matrix products  67.2 us (12%)
  other arithmetic  37.8 us (7%)
  between operations  14.1 us (3%)
    ppermute x3, waiting for transfers between devices, on_device(): lax.ppermute(held, 'patch', [(i, (i + 1) % count_2) for i in range(count_...  165 us
    psum x1, waiting for transfers between devices, spread(): return lax.psum(jnp.where(mine, array, jnp.zeros_like(array)), axis)  143 us
    ppermute x1, waiting for transfers between devices, passed_along(): lax.ppermute(value, axis, [(source, source + steps) for source in range(f...  49.4 us
    unnamed x37, local copies, waits for them, and re-layouts  25.6 us
    dot_general x2, matrix products, attend_one(): jnp.einsum('hqk,khe->qhe', weights, values, preferred_element_type=jnp.fl...  21.8 us
    dot_general x2, matrix products, attend_one(): jnp.einsum('qhe,khe->hqk', query, keys, preferred_element_type=jnp.float32)  19.3 us
    dot_general x1, matrix products, run_layer(): jnp.einsum('rid,dc->ric', normed, w_qkv, preferred_element_type=jnp.float32)  16.5 us
    concatenate x1, other arithmetic, run_layer(): keys_all = jnp.concatenate([text_one, mixed], 1)  13.1 us
  transfers between devices with their start and end apart: 7, of which 5 were waited for; matrix products, arithmetic and copies ran while one was open for 7% of the time, Pallas kernels for 0%

profile of v1, /device:TPU:1, one launch (start us, length us, event | category | flops | bytes accessed | tf_op | source)
XLA Modules:
  0.0 556.2 jit_solution(1447221498787377249)
XLA Ops:
  7.2 0.0 all-gather.7.cloned.1.call-start
  7.2 0.7 all-gather.7.cloned.1.call-update
  7.9 0.0 all-gather.5.cloned.1.call-start
  8.0 0.7 all-gather.5.cloned.1.call-update
  8.7 0.0 all-reduce.2.cloned.1.call-start
  8.7 3.2 copy.28
  11.9 2.2 collective-permute-start
  14.1 55.1 %collective-permute-done = bf16[2,256,2432]{1,2,0:T(8,128)(2,1)S(1)} collective-permute-done((bf16[2,256,2432]{1,2,0:T(8,128)(2,1)S(1)}, bf16[2,256,2432]{1,2,0:T(8,128)(2,1)S(1)}, u32[]{:S(2)}, u32[]{:S(2)}) %collective-permute-start) | collective-permute-done | bytes 2490400 | tf_op jit(solution)/shard_map/ppermute | solution.py:98
  69.2 1.4 copy-done.7
  70.6 55.5 %collective-permute-done.1 = bf16[2,256,2432]{1,2,0:T(8,128)(2,1)} collective-permute-done((bf16[2,256,2432]{1,2,0:T(8,128)(2,1)S(1)}, bf16[2,256,2432]{1,2,0:T(8,128)(2,1)}, u32[]{:S(2)}, u32[]{:S(2)}) %collective-permute-start.1) | collective-permute-done | bytes 2490400 | tf_op jit(solution)/shard_map/ppermute | solution.py:98
  126.1 54.8 %collective-permute-done.2 = bf16[2,256,2432]{1,2,0:T(8,128)(2,1)} collective-permute-done((bf16[2,256,2432]{1,2,0:T(8,128)(2,1)}, bf16[2,256,2432]{1,2,0:T(8,128)(2,1)}, u32[]{:S(2)}, u32[]{:S(2)}) %collective-permute-start.2) | collective-permute-done | bytes 2490400 | tf_op jit(solution)/shard_map/ppermute | solution.py:98
  180.9 3.6 constant_dynamic-update-slice_fusion.11
  184.5 3.5 constant_dynamic-update-slice_fusion.10
  188.0 1.7 constant_dynamic-update-slice_fusion.9
  189.7 1.7 constant_dynamic-update-slice_fusion.8
  191.3 3.4 constant_dynamic-update-slice_fusion.7
  194.7 3.4 constant_dynamic-update-slice_fusion.6
  198.1 1.6 constant_dynamic-update-slice_fusion.5
  199.7 1.7 constant_dynamic-update-slice_fusion.4
  201.5 8.9 %constant_dynamic-slice_fusion = bf16[2,1024,2432]{1,2,0:T(8,128)(2,1)} fusion(bf16[2,2048,2432]{1,2,0:T(8,128)(2,1)} %constant_dynamic-update-slice_fusion.4, s32[]{:T(128)S(6)} %select_n.40), kind=kLoop, calls=%fused_computation.126 | loop fusion | bytes 19922948 | tf_op jit(solution)/shard_map/jit(_roll_dynamic)/dynamic_slice | solution.py:101
  210.4 129.7 %conditional.2 = (bf16[2,256,2432]{2,1,0:T(8,128)(2,1)S(1)}, bf16[2,256,2432]{2,1,0:T(8,128)(2,1)}) conditional(s32[]{:T(128)} %convert_element_type.88, bf16[2,256,2432]{2,1,0:T(8,128)(2,1)S(1)} %copy-done.2, (bf16[2,256,2432]{2,1,0:T(8,128)(2,1)S(1)}, f32[1,2,3,2432]{3,1,2,0:T(2,128)S(1)}, bf16[2432,3648]{1,0:T(8,128)(2,1)}, f32[1,64]{1,0:T(1,128)S(1)}, ...), branch_computations={%region_0.1_spmd, %region_1.9_spmd} | conditional | flops 13646128128 | bytes 220811024 | solution.py:113
  210.6 0.4 convert_reduce_fusion
  211.0 0.8 fusion.15
  211.8 0.6 slice_bitcast_fusion.1
  212.4 16.5 %fusion.6 = f32[2,256,3648]{1,2,0:T(8,128)} fusion(bf16[2432,3648]{1,0:T(8,128)(2,1)} %get-tuple-element.139, bf16[2,256,2432]{2,1,0:T(8,128)(2,1)S(1)} %get-tuple-element.71, f32[2,2432]{1,0:T(2,128)S(1)} %get-tuple-element.182, f32[2,2432]{1,0:T(2,128)S(1)} %get-tuple-element.183, f32[2,256]{1,0:T(2,128)S(1)} %add_rsqrt_fusion.2, ...), kind=kOutput, calls=%fused_computation.11 | convolution fusion | flops 9092333568 | bytes 27748352 | tf_op jit(solution)/shard_map/cond/branch_1_fun/rid,dc->ric/dot_general | solution.py:55
  229.0 3.3 slice_multiply_fusion
  232.3 2.0 reduce_sum.99
  234.3 4.6 fusion.76
  238.9 2.9 slice.91
  241.8 8.8 %copy.62 = bf16[2,1024,2432]{1,2,0:T(8,128)(2,1)} copy(bf16[2,1024,2432]{1,2,0:T(8,128)(2,1)} %get-tuple-element.74) | data formatting | bytes 19922944 | tf_op jit(solution)/shard_map/cond
  250.6 4.3 pad_maximum_fusion.1
  254.9 5.8 %copy.30 = bf16[1,2,154,2432]{2,3,1,0:T(8,128)(2,1)} copy(bf16[1,2,154,2432]{3,1,2,0:T(2,128)(2,1)} %get-tuple-element.141) | data formatting | bytes 2996224 | tf_op jit(solution)/shard_map
  260.7 13.1 %pad_maximum_fusion = bf16[2,1178,2432]{1,2,0:T(8,128)(2,1)} fusion(bf16[2,1024,2432]{1,2,0:T(8,128)(2,1)} %get-tuple-element.180, bf16[2,154,2432]{1,2,0:T(8,128)(2,1)} %bitcast.148), kind=kLoop, calls=%fused_computation.13 | loop fusion | flops 22919168 | bytes 22919168 | tf_op jit(solution)/shard_map/cond/branch_1_fun/concatenate | solution.py:66
  273.8 0.3 multiply_reduce_fusion
  274.2 1.5 multiply_convert_fusion
  275.7 52.1 %while.18 = (s32[]{:T(128)}, bf16[2,256,1216]{1,2,0:T(8,128)(2,1)}, bf16[2,1178,2432]{1,2,0:T(8,128)(2,1)}, bf16[2,256,19,64]{1,3,2,0:T(8,128)(2,1)}, s32[]{:T(128)}) while((s32[]{:T(128)}, bf16[2,256,1216]{1,2,0:T(8,128)(2,1)}, bf16[2,1178,2432]{1,2,0:T(8,128)(2,1)}, bf16[2,256,19,64]{1,3,2,0:T(8,128)(2,1)}, s32[]{:T(128)}) %tuple.88), condition=%wide.region_8.8_spmd, body=%wide.region_6.7_spmd.sunk | while | flops 1478904064 | bytes 82245984 | solution.py:71
  275.9 3.2 dynamic-slice_bitcast_fusion.5
  279.1 0.4 fusion.96
  279.5 0.9 copy-done.5
  280.4 9.7 %exponential_reduce_fusion.5 = (f32[19,256]{1,0:T(8,128)S(1)}, f32[19,256,1178]{1,2,0:T(8,128)}) fusion(bf16[1178,19,64]{0,2,1:T(8,128)(2,1)S(1)} %bitcast.136, bf16[2,256,19,64]{1,3,2,0:T(8,128)(2,1)S(1)} %copy-done.5, s32[]{:T(128)} %get-tuple-element.287), kind=kOutput, calls=%fused_computation.clone.1 | convolution fusion | flops 739138304 | bytes 26674180 | tf_op jit(solution)/shard_map/cond/branch_1_fun/while/body/eval_jaxpr/qhe,khe->hqk/dot_general | solution.py:40
  290.0 10.9 %divide_convert_fusion.5 = bf16[256,19,64]{0,2,1:T(8,128)(2,1)S(1)} fusion(bf16[1178,19,64]{0,2,1:T(8,128)(2,1)S(1)} %bitcast.138, f32[19,256,1178]{1,2,0:T(8,128)} %get-tuple-element.265, f32[256,19]{0,1:T(8,128)S(1)} %bitcast.151), kind=kOutput, calls=%fused_computation.5.clone.1 | convolution fusion | flops 739765760 | bytes 26426112 | tf_op jit(solution)/shard_map/cond/branch_1_fun/while/body/eval_jaxpr/hqk,khe->qhe/dot_general | solution.py:44
  300.9 0.9 constant_dynamic-update-slice_fusion.15
  301.8 3.2 dynamic-slice_bitcast_fusion.5
  305.0 0.4 fusion.96
  305.4 0.9 copy-done.5
  306.3 9.7 %exponential_reduce_fusion.5 = (f32[19,256]{1,0:T(8,128)S(1)}, f32[19,256,1178]{1,2,0:T(8,128)}) fusion(bf16[1178,19,64]{0,2,1:T(8,128)(2,1)S(1)} %bitcast.136, bf16[2,256,19,64]{1,3,2,0:T(8,128)(2,1)S(1)} %copy-done.5, s32[]{:T(128)} %get-tuple-element.287), kind=kOutput, calls=%fused_computation.clone.1 | convolution fusion | flops 739138304 | bytes 26674180 | tf_op jit(solution)/shard_map/cond/branch_1_fun/while/body/eval_jaxpr/qhe,khe->hqk/dot_general | solution.py:40
  316.0 10.9 %divide_convert_fusion.5 = bf16[256,19,64]{0,2,1:T(8,128)(2,1)S(1)} fusion(bf16[1178,19,64]{0,2,1:T(8,128)(2,1)S(1)} %bitcast.138, f32[19,256,1178]{1,2,0:T(8,128)} %get-tuple-element.265, f32[256,19]{0,1:T(8,128)S(1)} %bitcast.151), kind=kOutput, calls=%fused_computation.5.clone.1 | convolution fusion | flops 739765760 | bytes 26426112 | tf_op jit(solution)/shard_map/cond/branch_1_fun/while/body/eval_jaxpr/hqk,khe->qhe/dot_general | solution.py:44
  326.9 0.9 constant_dynamic-update-slice_fusion.15
  327.8 7.6 %fusion.19 = bf16[2,256,2432]{2,1,0:T(8,128)(2,1)S(1)} fusion(bf16[2,256,2432]{2,1,0:T(8,128)(2,1)S(1)} %get-tuple-element.71, bf16[2,256,1216]{1,2,0:T(8,128)(2,1)} %get-tuple-element.78, bf16[1216,2432]{0,1:T(8,128)(2,1)} %get-tuple-element.144, f32[2,2432]{1,0:T(2,128)S(1)} %copy-done.12), kind=kOutput, calls=%fused_computation.26 | convolution fusion | flops 3033268224 | bytes 12160000 | tf_op jit(solution)/shard_map/cond/branch_1_fun/riw,wd->rid/dot_general | solution.py:72
  335.4 4.3 copy.46
  340.1 1.5 copy-done.1
  341.6 1.4 collective-permute-start.3
  343.0 0.6 divide_subtract_fusion
  343.7 0.6 copy_bitcast_fusion
  344.3 49.4 %collective-permute-done.3 = bf16[2,256,2432]{2,1,0:T(8,128)(2,1)S(1)} collective-permute-done((bf16[2,256,2432]{2,1,0:T(8,128)(2,1)}, bf16[2,256,2432]{2,1,0:T(8,128)(2,1)S(1)}, u32[]{:S(2)}, u32[]{:S(2)}) %collective-permute-start.3) | collective-permute-done | bytes 2490400 | tf_op jit(solution)/shard_map/ppermute | solution.py:16
  393.7 4.3 conditional.3
  393.7 1.6 broadcast.162.clone
  398.1 0.4 convert_reduce_fusion.2
  398.5 0.8 fusion.60
  399.3 1.8 fusion.69
  401.1 0.0 all-reduce.2.cloned.1.call-update
  401.2 3.4 select_bitcast_fusion
  404.6 143.3 %all-reduce.2.cloned.1.call-done = bf16[2,256,64]{1,2,0:T(8,128)(2,1)} async-done(((bf16[2,256,64]{1,2,0:T(8,128)(2,1)}), bf16[2,256,64]{1,2,0:T(8,128)(2,1)}) %all-reduce.2.cloned.1.call-update) | async-done | bytes 65552 | tf_op jit(solution)/shard_map/psum | solution.py:21
  548.0 1.5 fusion.73
  (44 shorter events, 0.2 us)
Async XLA Ops:
  7.2 392.1 %copy-start = (bf16[2432,64]{0,1:T(8,128)(2,1)S(1)}, bf16[2432,64]{0,1:T(8,128)(2,1)}, u32[]{:S(2)}) copy-start(bf16[2432,64]{0,1:T(8,128)(2,1)} %param.27) | copy-start | bytes 933892
  7.2 203.2 %all-gather.7.cloned.1.call-start = ((), (), s32[]{:S(2)}) async-start(), calls=%async_computation.2 | async-start | bytes 6615040 | tf_op jit(solution)/shard_map/all_gather | solution.py:92
  7.9 202.4 %all-gather.5.cloned.1.call-start = ((), (), s32[]{:S(2)}) async-start(), calls=%async_computation.1 | async-start | bytes 19183616 | tf_op jit(solution)/shard_map/all_gather | solution.py:91
  8.7 539.3 %all-reduce.2.cloned.1.call-start = ((), (), s32[]{:S(2)}) async-start(), calls=%async_computation | async-start | bytes 131072 | tf_op jit(solution)/shard_map/psum | solution.py:21
  11.9 57.3 %collective-permute-start = (bf16[2,256,2432]{1,2,0:T(8,128)(2,1)S(1)}, bf16[2,256,2432]{1,2,0:T(8,128)(2,1)S(1)}, u32[]{:S(2)}, u32[]{:S(2)}) collective-permute-start(bf16[2,256,2432]{1,2,0:T(8,128)(2,1)S(1)} %bitcast.142), channel_id=1, source_target_pairs={{0,16},{16,32},{32,48},{48,0},{1,17},{17,33},{33,49},{49,1},{2,18}... | collective-permute-start | bytes 7471112 | tf_op jit(solution)/shard_map/ppermute | solution.py:98
  69.2 1.4 copy-start.7
  70.6 55.5 %collective-permute-start.1 = (bf16[2,256,2432]{1,2,0:T(8,128)(2,1)S(1)}, bf16[2,256,2432]{1,2,0:T(8,128)(2,1)}, u32[]{:S(2)}, u32[]{:S(2)}) collective-permute-start(bf16[2,256,2432]{1,2,0:T(8,128)(2,1)S(1)} %collective-permute-done), channel_id=1, source_target_pairs={{0,16},{16,32},{32,48},{48,0},{1,17},{17,33},{33,49},{49,1},{2,18}... | collective-permute-start | bytes 7471112 | tf_op jit(solution)/shard_map/ppermute | solution.py:98
  126.1 54.8 %collective-permute-start.2 = (bf16[2,256,2432]{1,2,0:T(8,128)(2,1)}, bf16[2,256,2432]{1,2,0:T(8,128)(2,1)}, u32[]{:S(2)}, u32[]{:S(2)}) collective-permute-start(bf16[2,256,2432]{1,2,0:T(8,128)(2,1)} %collective-permute-done.1), channel_id=1, source_target_pairs={{0,16},{16,32},{32,48},{48,0},{1,17},{17,33},{33,49},{49,1},{2,18}... | collective-permute-start | bytes 7471112 | tf_op jit(solution)/shard_map/ppermute | solution.py:98
  184.5 3.5 copy-start.8
  201.5 8.9 %copy-start.2 = (bf16[2,256,2432]{2,1,0:T(8,128)(2,1)S(1)}, bf16[2,256,2432]{2,1,0:T(8,128)(2,1)}, u32[]{:S(2)}) copy-start(bf16[2,256,2432]{2,1,0:T(8,128)(2,1)} %param.19) | copy-start | bytes 7471108
  201.5 8.9 %copy-start.9 = (f32[1,2,3,2432]{3,1,2,0:T(2,128)S(1)}, f32[1,2,3,2432]{3,1,2,0:T(2,128)}, u32[]{:S(2)}) copy-start(f32[1,2,3,2432]{3,1,2,0:T(2,128)} %param.22) | copy-start | bytes 175108
  201.5 8.9 %copy-start.16 = (f32[1,64]{1,0:T(1,128)S(1)}, f32[1,64]{1,0:T(1,128)}, u32[]{:S(2)}) copy-start(f32[1,64]{1,0:T(1,128)} %param.23) | copy-start | bytes 772
  210.4 132.7 %copy-start.19 = (s32[2]{0:T(128)S(1)}, s32[2]{0:T(128)}, u32[]{:S(2)}) copy-start(s32[2]{0:T(128)} %param.29) | copy-start | bytes 28
  210.4 133.3 %copy-start.11 = (f32[2,2,2432]{2,1,0:T(2,128)S(1)}, f32[2,2,2432]{2,1,0:T(2,128)}, u32[]{:S(2)}) copy-start(f32[2,2,2432]{2,1,0:T(2,128)} %param.26) | copy-start | bytes 116740
  260.7 13.1 %copy-start.3 = (f32[2,256,1216]{1,2,0:T(8,128)S(1)}, f32[2,256,1216]{1,2,0:T(8,128)}, u32[]{:S(2)}) copy-start(f32[2,256,1216]{1,2,0:T(8,128)} %get-tuple-element.177) | copy-start | bytes 7471108 | tf_op jit(solution)/shard_map/cond
  275.7 52.1 %copy-start.12 = (f32[2,2432]{1,0:T(2,128)S(1)}, f32[2,2432]{1,0:T(2,128)}, u32[]{:S(2)}) copy-start(f32[2,2432]{1,0:T(2,128)} %get-tuple-element.181) | copy-start | bytes 58372 | tf_op jit(solution)/shard_map/cond
  279.1 1.3 copy-start.5
  305.0 1.3 copy-start.5
  340.1 1.5 copy-start.1
  341.6 52.1 %collective-permute-start.3 = (bf16[2,256,2432]{2,1,0:T(8,128)(2,1)}, bf16[2,256,2432]{2,1,0:T(8,128)(2,1)S(1)}, u32[]{:S(2)}, u32[]{:S(2)}) collective-permute-start(bf16[2,256,2432]{2,1,0:T(8,128)(2,1)} %copy-done.1), channel_id=1, source_target_pairs={{0,64},{1,65},{2,66},{3,67},{4,68},{5,69},{6,70},{7,71},{8,72},{9,... | collective-permute-start | bytes 7471112 | tf_op jit(solution)/shard_map/ppermute | solution.py:16
  398.0 1.2 copy-start.14
  398.0 1.2 copy-start.15
  401.2 146.8 %copy-start.10 = (f32[2,128,64]{1,2,0:T(8,128)S(1)}, f32[2,128,64]{1,2,0:T(8,128)}, u32[]{:S(2)}) copy-start(f32[2,128,64]{1,2,0:T(8,128)} %param.28) | copy-start | bytes 196612
  401.2 146.8 %copy-start.17 = (f32[2]{0:T(128)S(1)}, f32[2]{0:T(128)}, u32[]{:S(2)}) copy-start(f32[2]{0:T(128)} %get-tuple-element.171) | copy-start | bytes 28
  401.2 146.8 %copy-start.18 = (f32[2]{0:T(128)S(1)}, f32[2]{0:T(128)}, u32[]{:S(2)}) copy-start(f32[2]{0:T(128)} %get-tuple-element.172) | copy-start | bytes 28
Sparse Core Ops, SparseCore 0:
  10.4 67.5 all-gather.6
  80.5 114.4 all-gather.4
  401.3 146.6 all-reduce.1
